TPU v7x, 256 devices: a whole 4x4x8 slice. The times are simulated.
256 devices in a mesh: sub: 32 (over z_hi, y, core), grp: 8 (over z_lo, x).
Axes of the slice: x: 4, y: 4, z: 8 (z_hi: 4, z_lo: 2; z = z_hi * 2 + z_lo), core: 2. Of those that a mesh axis runs over, the one named last changes fastest.
Arguments:
- right_side: float32 [8, 32, 1024, 128], P('grp', 'sub'), may hold values from -13 to 13
- schur_blocks: bfloat16 [8, 32, 2048, 2048], P('grp', 'sub'), may hold values from -2 to 7, as said below
- occupancy: int32 [8, 32, 1024], P('grp', 'sub'), may hold values 0 or 1
- precond_weights: float32 [8, 32, 1024], P('grp', 'sub'), may hold values from 0.1 to 1
- coarse_basis: float32 [8, 32, 8, 1024], P('grp', 'sub'), may hold values from -0.1875 to 0.1875
- coarse_inverse: float32 [8, 256, 256], P('grp', 'sub'), may hold values from -1 to 5, as said below
Outputs:
- solution: float32 [8, 32, 1024, 128], P('grp', 'sub')
- residual: float32 [8, 32, 1024, 128], P('grp', 'sub')
Inputs may be any that keep to these rules, and one draw needn't show every extreme that they name: `schur_blocks`: each strip's block is symmetric positive definite, diagonal entries between 1.4 and 6.1. `coarse_inverse`: each group's matrix is symmetric positive definite, diagonal entries between 0.9 and 4.2.
All inputs are finite; a program needn't handle non-finite values. No bound on the sum of `occupancy` on one device may be relied on, other than what follows from the above.
Results may differ from a plain program's by a relative error of at most 0.035.
Values may be sent and summed in bfloat16 or wider, within the bound.
A program may use at most 64 MiB of HBM per device.

v0:
```python
import jax
import jax.numpy as jnp
from jax import lax
from jax.sharding import PartitionSpec as P

ITERS = 3


def passed_along(block, axis, distance):
    devices = range(lax.axis_size(axis))
    route = [((i - distance) % len(devices), i) for i in devices]
    return lax.ppermute(block, axis, route)


def shifted(value, axis, steps):
    count = lax.axis_size(axis)
    initial, last = (max(0, -steps), min(count, count - steps))
    return lax.ppermute(value, axis, [(source, source + steps) for source in range(initial, last)])


def local(right_side, schur_blocks, occupancy, precond_weights, coarse_basis, coarse_inverse):
    schur_block = schur_blocks[0, 0]
    free_cells = occupancy[0, 0].astype(jnp.float32)[:, None]
    weight_col = precond_weights[0, 0][:, None]
    basis_rows = coarse_basis[0, 0]
    inverse_rows = coarse_inverse[0]
    source = right_side[0, 0]
    face_cells = source.shape[0]
    group_count = lax.axis_size("sub")
    position = lax.axis_index("sub")
    contract = (((0,), (0,)), ((), ()))

    def precondition(residual):
        coarse = jnp.dot(basis_rows, residual, precision=lax.Precision.HIGHEST)
        group_coarse = lax.all_gather(coarse, "sub", axis=0, tiled=True)
        solved = jnp.dot(inverse_rows, group_coarse, precision=lax.Precision.HIGHEST)
        spread_back = lax.dot_general(basis_rows, solved, contract, precision=lax.Precision.HIGHEST)
        return weight_col * residual + spread_back

    def precond_inner(residual, precond):
        return lax.psum(jnp.sum(residual * precond, axis=0), ("sub", "grp"))

    solution = jnp.zeros_like(source)
    residual = source
    precond = precondition(residual)
    direction = precond
    inner_now = precond_inner(residual, precond)
    for iteration in range(ITERS):
        masked = (free_cells * direction).astype(jnp.bfloat16)
        beside_all = passed_along(masked, "sub", -1)
        crossed = shifted(beside_all, "grp", -1)
        following = jnp.where(position == group_count - 1, crossed, beside_all)
        stacked = jnp.concatenate([masked, following], axis=0)
        product = jnp.dot(schur_block, stacked, preferred_element_type=jnp.float32)
        outgoing = product[face_cells:].astype(jnp.bfloat16)
        behind = passed_along(outgoing, "sub", 1)
        crossed_back = shifted(behind, "grp", 1)
        incoming = jnp.where(position == 0, crossed_back, behind)
        image = (
            free_cells * (product[:face_cells] + incoming.astype(jnp.float32))
            + (1.0 - free_cells) * direction
        )
        step_size = inner_now / lax.psum(jnp.sum(direction * image, axis=0), ("sub", "grp"))
        solution = solution + step_size * direction
        residual = residual - step_size * image
        if iteration + 1 < ITERS:
            precond = precondition(residual)
            inner_next = precond_inner(residual, precond)
            direction = precond + inner_next / inner_now * direction
            inner_now = inner_next
    return (solution[None, None], residual[None, None])


def solution(mesh):
    return jax.shard_map(
        local,
        mesh=mesh,
        in_specs=(
            P("grp", "sub", None, None),
            P("grp", "sub", None, None),
            P("grp", "sub", None),
            P("grp", "sub", None),
            P("grp", "sub", None, None),
            P("grp", "sub", None),
        ),
        out_specs=(P("grp", "sub", None, None), P("grp", "sub", None, None)),
        check_vma=False,
    )
```

profile of v0, /device:TPU:1, one launch (start us, length us, event | category | flops | bytes accessed | tf_op | source)
XLA Modules:
  0.0 647.4 jit_solution(17180566580435164239)
XLA Ops:
  0.6 0.0 copy-start
  0.6 0.7 convert_element_type.34
  1.3 1.2 copy.11
  2.6 0.0 copy-done
  2.6 1.4 fusion.33
  4.0 49.2 %all_gather.9 = f32[256,128]{1,0:T(8,128)S(1)} all-gather(f32[8,128]{1,0:T(8,128)S(1)} %fusion.33), channel_id=1, replica_groups=mesh['sub'=32,'grp'=8] {'sub'}, dimensions={0}, use_global_device_ids=true | all-gather | bytes 135168 | tf_op jit(solution)/shard_map/all_gather | solution.py:35
  53.2 1.1 fusion.46
  54.3 1.3 multiply_convert_fusion.2
  55.6 0.0 copy-start.3
  55.6 0.2 collective-permute-start
  55.8 5.6 collective-permute-done
  61.5 1.3 collective-permute-start.1
  62.8 0.0 copy-start.4
  62.8 7.3 %collective-permute-done.1 = bf16[1024,128]{0,1:T(8,128)(2,1)S(1)} collective-permute-done((bf16[1024,128]{0,1:T(8,128)(2,1)S(1)}, bf16[1024,128]{0,1:T(8,128)(2,1)S(1)}, u32[]{:S(2)}, u32[]{:S(2)}) %collective-permute-start.1) | collective-permute-done | bytes 262176 | tf_op jit(solution)/shard_map/ppermute | solution.py:18
  70.1 6.2 fusion.6
  76.4 0.1 collective-permute-start.2
  76.5 3.3 collective-permute-done.2
  79.8 3.1 collective-permute-start.3
  83.0 3.3 collective-permute-done.3
  86.2 0.3 multiply_reduce_fusion.4
  86.5 86.7 %all-reduce = (f32[128]{0:T(128)S(1)}, f32[128]{0:T(128)S(1)}) all-reduce(f32[128]{0:T(128)S(1)} %get-tuple-element.7, f32[128]{0:T(128)S(1)} %get-tuple-element.6), channel_id=1, replica_groups=mesh['sub'=32,'grp'=8] {'sub','grp'}, use_global_device_ids=true, to_apply=%region_1.0 | all-reduce | flops 256 | bytes 2048 | tf_op jit(solution)/shard_map/psum | solution.py:41
  173.2 0.2 bitcast_subtract_fusion
  173.4 0.5 convolution_bitcast_fusion.4
  173.9 41.9 %all_gather.10 = f32[256,128]{1,0:T(8,128)S(1)} all-gather(f32[8,128]{1,0:T(8,128)S(1)} %convolution_bitcast_fusion.4), channel_id=1, replica_groups=mesh['sub'=32,'grp'=8] {'sub'}, dimensions={0}, use_global_device_ids=true | all-gather | bytes 135168 | tf_op jit(solution)/shard_map/all_gather | solution.py:35
  215.8 0.0 copy-done.3
  215.8 0.4 fusion.44
  216.2 0.0 copy-done.4
  216.2 0.7 multiply_reduce_fusion.3
  216.9 72.9 %psum.44 = f32[128]{0:T(128)S(1)} all-reduce(f32[128]{0:T(128)S(1)} %get-tuple-element.18), channel_id=1, replica_groups=mesh['sub'=32,'grp'=8] {'sub','grp'}, use_global_device_ids=true, to_apply=%region_5.6 | all-reduce | flops 128 | bytes 1024 | tf_op jit(solution)/shard_map/psum | solution.py:41
  289.8 0.1 multiply_convert_fusion.1
  289.9 0.8 collective-permute-start.4
  290.7 5.1 collective-permute-done.4
  295.8 1.3 collective-permute-start.5
  297.1 7.1 %collective-permute-done.5 = bf16[1024,128]{0,1:T(8,128)(2,1)S(1)} collective-permute-done((bf16[1024,128]{0,1:T(8,128)(2,1)S(1)}, bf16[1024,128]{0,1:T(8,128)(2,1)S(1)}, u32[]{:S(2)}, u32[]{:S(2)}) %collective-permute-start.5) | collective-permute-done | bytes 262176 | tf_op jit(solution)/shard_map/ppermute | solution.py:18
  304.2 6.3 fusion.9
  310.5 2.7 collective-permute-start.6
  313.2 3.3 collective-permute-done.6
  316.5 2.1 collective-permute-start.7
  318.6 3.3 collective-permute-done.7
  321.9 0.2 multiply_reduce_fusion.2
  322.1 84.7 %psum.45 = f32[128]{0:T(128)S(1)} all-reduce(f32[128]{0:T(128)S(1)} %multiply_reduce_fusion.2), channel_id=1, replica_groups=mesh['sub'=32,'grp'=8] {'sub','grp'}, use_global_device_ids=true, to_apply=%region_7.8 | all-reduce | flops 128 | bytes 1024 | tf_op jit(solution)/shard_map/psum | solution.py:63
  406.8 0.0 copy-done.1
  406.8 0.2 multiply_subtract_fusion
  406.9 0.5 convolution_bitcast_fusion.3
  407.5 43.1 %all_gather.11 = f32[256,128]{1,0:T(8,128)S(1)} all-gather(f32[8,128]{1,0:T(8,128)S(1)} %convolution_bitcast_fusion.3), channel_id=1, replica_groups=mesh['sub'=32,'grp'=8] {'sub'}, dimensions={0}, use_global_device_ids=true | all-gather | bytes 135168 | tf_op jit(solution)/shard_map/all_gather | solution.py:35
  450.6 0.4 fusion.42
  451.0 0.7 multiply_reduce_fusion.1
  451.7 72.9 %psum.46 = f32[128]{0:T(128)S(1)} all-reduce(f32[128]{0:T(128)S(1)} %get-tuple-element.20), channel_id=1, replica_groups=mesh['sub'=32,'grp'=8] {'sub','grp'}, use_global_device_ids=true, to_apply=%region_9.10 | all-reduce | flops 128 | bytes 1024 | tf_op jit(solution)/shard_map/psum | solution.py:41
  524.6 0.1 multiply_convert_fusion
  524.7 0.9 collective-permute-start.8
  525.6 4.9 collective-permute-done.8
  530.6 1.3 collective-permute-start.9
  531.9 8.7 %collective-permute-done.9 = bf16[1024,128]{0,1:T(8,128)(2,1)S(1)} collective-permute-done((bf16[1024,128]{0,1:T(8,128)(2,1)S(1)}, bf16[1024,128]{0,1:T(8,128)(2,1)S(1)}, u32[]{:S(2)}, u32[]{:S(2)}) %collective-permute-start.9) | collective-permute-done | bytes 262176 | tf_op jit(solution)/shard_map/ppermute | solution.py:18
  540.6 6.3 fusion.12
  546.9 0.2 collective-permute-start.10
  547.1 3.3 collective-permute-done.10
  550.4 2.0 collective-permute-start.11
  552.4 3.3 collective-permute-done.11
  555.7 0.7 copy-done.2
  556.4 0.2 multiply_reduce_fusion
  556.6 85.4 %psum.47 = f32[128]{0:T(128)S(1)} all-reduce(f32[128]{0:T(128)S(1)} %multiply_reduce_fusion), channel_id=1, replica_groups=mesh['sub'=32,'grp'=8] {'sub','grp'}, use_global_device_ids=true, to_apply=%region_11.12 | all-reduce | flops 128 | bytes 1024 | tf_op jit(solution)/shard_map/psum | solution.py:63
  642.1 1.3 subtract_bitcast_fusion
  643.3 2.0 copy.13
  645.4 2.0 copy.12
  (14 shorter events, 0.2 us)
Async XLA Ops:
  0.6 2.0 copy-start
  55.6 160.2 %copy-start.3 = (f32[1,8,256]{2,1,0:T(8,128)S(1)}, f32[1,8,256]{2,1,0:T(8,128)}, u32[]{:S(2)}) copy-start(f32[1,8,256]{2,1,0:T(8,128)} %param.11) | copy-start | bytes 24580
  55.6 5.9 collective-permute-start
  61.5 8.6 %collective-permute-start.1 = (bf16[1024,128]{0,1:T(8,128)(2,1)S(1)}, bf16[1024,128]{0,1:T(8,128)(2,1)S(1)}, u32[]{:S(2)}, u32[]{:S(2)}) collective-permute-start(bf16[1024,128]{0,1:T(8,128)(2,1)S(1)} %collective-permute-done), channel_id=1, source_target_pairs={{1,0},{2,1},{3,2},{4,3},{5,4},{6,5},{7,6},{9,8},{10,9},{11,10},{12... | collective-permute-start | bytes 786440 | tf_op jit(solution)/shard_map/ppermute | solution.py:18
  62.8 153.4 %copy-start.4 = (f32[1,1,1024]{2,1,0:T(1,128)S(1)}, f32[1,1,1024]{2,1,0:T(1,128)}, u32[]{:S(2)}) copy-start(f32[1,1,1024]{2,1,0:T(1,128)} %param.9) | copy-start | bytes 12292
  76.4 3.4 collective-permute-start.2
  79.8 6.4 collective-permute-start.3
  289.9 5.9 collective-permute-start.4
  295.8 8.4 %collective-permute-start.5 = (bf16[1024,128]{0,1:T(8,128)(2,1)S(1)}, bf16[1024,128]{0,1:T(8,128)(2,1)S(1)}, u32[]{:S(2)}, u32[]{:S(2)}) collective-permute-start(bf16[1024,128]{0,1:T(8,128)(2,1)S(1)} %collective-permute-done.4), channel_id=1, source_target_pairs={{1,0},{2,1},{3,2},{4,3},{5,4},{6,5},{7,6},{9,8},{10,9},{11,10},{12... | collective-permute-start | bytes 786440 | tf_op jit(solution)/shard_map/ppermute | solution.py:18
  310.5 6.0 collective-permute-start.6
  316.5 5.4 collective-permute-start.7
  321.9 84.9 %copy-start.1 = (bf16[1024,128]{0,1:T(8,128)(2,1)}, bf16[1024,128]{0,1:T(8,128)(2,1)S(1)}, u32[]{:S(2)}) copy-start(bf16[1024,128]{0,1:T(8,128)(2,1)S(1)} %collective-permute-done.7) | copy-start | bytes 786436
  524.7 5.9 collective-permute-start.8
  530.6 9.9 %collective-permute-start.9 = (bf16[1024,128]{0,1:T(8,128)(2,1)S(1)}, bf16[1024,128]{0,1:T(8,128)(2,1)S(1)}, u32[]{:S(2)}, u32[]{:S(2)}) collective-permute-start(bf16[1024,128]{0,1:T(8,128)(2,1)S(1)} %collective-permute-done.8), channel_id=1, source_target_pairs={{1,0},{2,1},{3,2},{4,3},{5,4},{6,5},{7,6},{9,8},{10,9},{11,10},{12... | collective-permute-start | bytes 786440 | tf_op jit(solution)/shard_map/ppermute | solution.py:18
  546.9 3.5 collective-permute-start.10
  550.4 5.2 collective-permute-start.11
  555.7 0.7 copy-start.2
where the time goes:
time: 649 us; the launch traced here: 647 us
  blocking collectives  537 us (83%)
  waiting for transfers between devices  58.5 us (9%)
  matrix products  25.7 us (4%)
  starting transfers between devices  15.9 us (2%)
    psum x3, blocking collectives, precond_inner(): return lax.psum(jnp.sum(residual * precond, axis=0), ('sub', 'grp'))  232 us
    psum x2, blocking collectives, local(): lax.psum(jnp.sum(direction * image, axis=0), ('sub', 'grp'))  170 us
    all_gather x3, blocking collectives, precondition(): group_coarse = lax.all_gather(coarse, 'sub', axis=0, tiled=True)  134 us
    ppermute x6, waiting for transfers between devices, shifted(): lax.ppermute(value, axis, [(source, source + steps) for source in range(i...  32.9 us
    ppermute x6, waiting for transfers between devices, passed_along(): return lax.ppermute(block, axis, route)  25.6 us
    dot_general x3, matrix products, local(): product = jnp.dot(schur_block, stacked, preferred_element_type=jnp.float32)  18.8 us
  transfers between devices with their start and end apart: 12, of which 12 were waited for; matrix products, arithmetic and copies ran while one was open for 0% of the time, Pallas kernels for 0%

commit v1 on v0

v1 whole, which is shorter than its diff:
```python
import functools

import jax
import jax.numpy as jnp
from jax import lax
from jax.experimental import pallas as pl
from jax.experimental.pallas import tpu as pltpu
from jax.sharding import PartitionSpec as P

ITERS = 3
MESH = pl.DeviceIdType.MESH
F32 = jnp.float32
BF16 = jnp.bfloat16
CH = 256


def split(value):
    high = value.astype(BF16)
    return high, (value - high.astype(F32)).astype(BF16)


def folded(value):
    return jnp.sum(value.reshape(value.shape[0] // 8, 8, value.shape[1]), axis=0)


def place(row):
    return pl.ds(pl.multiple_of(row, CH), CH)


def kernel(
    n_sub, n_grp,
    b_hbm, s_hbm, occ_hbm, w_hbm, basis_hbm, inv_hbm,
    x_ref, r_ref,
    blocks, res, zed, srch, prod, weight, free, masked, held, arrive, leave, half_b,
    own_par, next_par, occ_v, inv, basis_t, spread_rhs, prob, qmat, basis_n, direc,
    coarse_src, coarse_all, kap_src, kap_in, dot_src, dot_grp, dot_mid, dot_sub,
    load_sem, send_sem, par_sem, half_sem, inv_sem, bulk_sem, kap_sem, all_sem, far_sem, grp_sem, sub_sem,
):
    s = lax.axis_index("sub")
    g = lax.axis_index("grp")
    face = b_hbm.shape[0]
    nc = basis_hbm.shape[0]
    goals = b_hbm.shape[1]
    last_s = n_sub - 1
    at_end = s == last_s
    next_s = lax.rem(s + 1, n_sub)
    next_g = lax.rem(g + jnp.where(at_end, 1, 0), n_grp)
    prev_s = lax.rem(s + n_sub - 1, n_sub)
    prev_g = lax.rem(g + jnp.where(s == 0, n_grp - 1, 0), n_grp)
    above_g = lax.rem(g + 1, n_grp)
    below_g = lax.rem(g + n_grp - 1, n_grp)
    has_next = jnp.where(jnp.logical_and(at_end, g == n_grp - 1), 0.0, 1.0).astype(F32)
    has_prev = jnp.where(jnp.logical_and(s == 0, g == 0), 0.0, 1.0).astype(F32)
    nxt = {"sub": next_s, "grp": next_g}
    prv = {"sub": prev_s, "grp": prev_g}

    def local(src, dst, i):
        return pltpu.make_async_copy(src, dst, load_sem.at[i])

    loads = [
        local(b_hbm, res.at[pl.ds(0, face)], 0),
        local(occ_hbm, occ_v, 1),
        local(w_hbm, own_par.at[pl.ds(nc, 1)], 2),
        local(basis_hbm, own_par.at[pl.ds(0, nc)], 3),
        local(inv_hbm, inv.at[0], 4),
        local(s_hbm, blocks, 5),
    ]
    for copy in loads:
        copy.start()

    barrier = pltpu.get_barrier_semaphore()

    def greet(sub, grp):
        pl.semaphore_signal(barrier, inc=1, device_id={"sub": sub, "grp": grp}, device_id_type=MESH)

    def greet_sub(j, carry):
        greet(lax.rem(s + j, n_sub), g)
        return carry

    def greet_grp(j, carry):
        greet(s, lax.rem(g + j, n_grp))
        return carry

    lax.fori_loop(1, n_sub, greet_sub, 0)
    lax.fori_loop(1, n_grp, greet_grp, 0)

    @pl.when(s != last_s)
    def _():
        greet(last_s, below_g)

    @pl.when(at_end)
    def _():
        def greet_above(j, carry):
            greet(j, above_g)
            return carry

        lax.fori_loop(0, last_s, greet_above, 0)

    def remote(src, dst, send, recv, sub, grp):
        return pltpu.make_async_remote_copy(
            src_ref=src, dst_ref=dst, send_sem=send, recv_sem=recv,
            device_id={"sub": sub, "grp": grp}, device_id_type=MESH,
        )

    def take(ref, sem):
        pltpu.make_async_copy(ref, ref, sem).wait()

    def gather_coarse(k, value):
        coarse_src[k] = value
        coarse_all[k, 0, pl.ds(s, 1)] = value[None]

        def one(j, carry):
            remote(coarse_src.at[k], coarse_all.at[k, 0, s], send_sem.at[0, k], all_sem.at[k], lax.rem(s + j, n_sub), g).start()
            return carry

        lax.fori_loop(1, n_sub, one, 0)
        remote(coarse_src.at[k], coarse_all.at[k, 1, s], send_sem.at[1, k], far_sem.at[k], last_s, below_g).start()

    def solve_coarse(k):
        take(coarse_all.at[k, 0, pl.ds(0, n_sub - 1)], all_sem.at[k])

        @pl.when(at_end)
        def _():
            take(coarse_all.at[k, 1], far_sem.at[k])

        own = coarse_all[k, 0].reshape(n_sub * nc, goals)
        beside = coarse_all[k, jnp.where(at_end, 1, 0)].reshape(n_sub * nc, goals)
        dot = functools.partial(jnp.dot, precision=lax.Precision.HIGHEST, preferred_element_type=F32)
        return dot(inv[0], own), dot(inv[1], beside)

    loads[0].wait()
    loads[1].wait()
    loads[2].wait()
    loads[3].wait()
    own_par[pl.ds(nc + 1, 1)] = occ_v[...].astype(F32)

    def split_rows(rows):
        high, low = split(rows)
        return jnp.concatenate([high, low], axis=0)

    own_basis = split_rows(own_par[0:nc])
    coarse = jnp.zeros((2 * nc, 2 * goals), F32)
    for row in range(0, face, CH):
        high, low = split(res[pl.ds(row, CH)])
        half_b[pl.ds(row, CH)] = high
        coarse += jnp.dot(own_basis[:, row:row + CH], jnp.concatenate([high, low], axis=1), preferred_element_type=F32)

    def unsplit(value, rows):
        both = value[:, :goals] + value[:, goals:]
        return both[:rows] + both[rows:]

    first_coarse = unsplit(coarse, nc)
    pl.semaphore_wait(barrier, (n_sub - 1) + (n_grp - 1) + jnp.where(at_end, n_sub - 1, 1))
    gather_coarse(0, first_coarse)
    remote(own_par, next_par, send_sem.at[2, 0], par_sem, prev_s, prev_g).start()
    loads[4].wait()
    remote(inv.at[0], inv.at[1], send_sem.at[3, 0], inv_sem, prev_s, prev_g).start()
    remote(half_b, held, send_sem.at[4, 0], half_sem, prev_s, prev_g).start()

    def prepare(base, params):
        high, low = split(params[0:nc])
        quad = jnp.concatenate([high, high, low, low], axis=0).astype(F32)
        for col in range(0, face, 128):
            span = pl.ds(base + col, 128)
            basis_t[span] = jnp.transpose(quad[:, col:col + 128]).astype(BF16)
            weight[span] = jnp.transpose(jnp.broadcast_to(params[nc:nc + 1, col:col + 128], (128, 128)))
            free[span] = jnp.transpose(jnp.broadcast_to(params[nc + 1:nc + 2, col:col + 128], (128, 128)))

    def through(base, params, which):
        rows = split_rows(params[0:nc] * params[nc + 1:nc + 2])
        for col in range(0, 2 * face, CH):
            out = jnp.dot(rows, blocks[pl.ds(base, face), pl.ds(col, CH)], preferred_element_type=F32)
            high, low = split(out[:nc] + out[nc:])
            qmat[which, 0:nc, pl.ds(col, CH)] = high
            qmat[which, nc:2 * nc, pl.ds(col, CH)] = low

    params = own_par[...]
    prepare(0, params)
    basis_n[...] = split_rows(params[0:nc] * (1.0 - params[nc + 1:nc + 2]))
    loads[5].wait()
    through(0, params, 0)
    take(next_par, par_sem)
    params = next_par[...] * has_next
    prepare(face, params)
    through(face, params, 1)
    take(inv.at[1], inv_sem)

    def stage_spread(which, value):
        high, low = split(value)
        spread_rhs[which] = jnp.concatenate([high, low, high, low], axis=0)

    def build(span, which, r):
        z = weight[span] * r + jnp.dot(basis_t[span], spread_rhs[which], preferred_element_type=F32)
        fz = free[span] * z
        high, low = split(fz)
        masked[span, 0:goals] = high
        masked[span, goals:2 * goals] = low
        zed[span] = z
        return z, fz

    zero8 = jnp.zeros((8, goals), F32)
    solved, solved_next = solve_coarse(0)
    stage_spread(0, solved)
    stage_spread(1, solved_next)

    def leftover(span, rest):
        high, low = split(rest)
        prob[span, 0:goals] = high
        prob[span, goals:2 * goals] = low

    def first_own(i, carry):
        gamma, delta = carry
        span = place(i * CH)
        r = res[span]
        z, fz = build(span, 0, r)
        rest = z - fz
        leftover(span, rest)
        return gamma + folded(r * z), delta + folded(rest * z)

    gamma, delta = lax.fori_loop(0, face // CH, first_own, (zero8, zero8))
    eps = zero8
    take(held, half_sem)

    def first_next(i, carry):
        span = place(face + i * CH)
        r = held[place(i * CH)].astype(F32) * has_next
        res[span] = r
        build(span, 1, r)
        return carry

    lax.fori_loop(0, face // CH, first_next, 0)

    gamma_old = p_ap = None
    drift = drift_next = None
    for k in range(ITERS):
        more = k + 1 < ITERS
        if more:
            m_all = masked[...]
            part = jnp.dot(qmat[0], m_all, preferred_element_type=F32)
            kap = jnp.dot(qmat[1], m_all, preferred_element_type=F32)
            part += jnp.dot(basis_n[...], prob[...], preferred_element_type=F32)
            kap_src[k] = unsplit(kap, nc)
            remote(kap_src.at[k], kap_in.at[k], send_sem.at[5, k], kap_sem.at[k], next_s, next_g).start()
            part = unsplit(part, nc)

        def rows_of(row, acc):
            span = place(row)
            y = jnp.dot(blocks[span], masked[...], preferred_element_type=F32)
            y = y[:, :goals] + y[:, goals:]
            prod[span] = y
            leave[k, span] = y.astype(BF16)
            return acc + folded(free[span] * zed[span] * y)

        def pair(i, acc):
            acc = rows_of(face + i * CH, acc)
            remote(
                leave.at[k, place(face + i * CH)], arrive.at[k, place(i * CH)],
                send_sem.at[6, k], bulk_sem.at[k, 0], next_s, next_g,
            ).start()
            acc = rows_of(i * CH, acc)
            if more:
                remote(
                    leave.at[k, place(i * CH)], arrive.at[k, place(face + i * CH)],
                    send_sem.at[7, k], bulk_sem.at[k, 1], prev_s, prev_g,
                ).start()
            return acc

        delta = lax.fori_loop(0, face // CH, pair, delta)
        dots = [jnp.sum(v, axis=0, keepdims=True) for v in (gamma, delta, eps)]
        dots = jnp.concatenate(dots + [jnp.zeros((1, goals), F32)], axis=0)
        dot_src[k] = dots
        dot_grp[k, pl.ds(g, 1)] = dots[None]

        def to_grp(j, carry):
            remote(dot_src.at[k], dot_grp.at[k, g], send_sem.at[8, k], grp_sem.at[k], s, lax.rem(g + j, n_grp)).start()
            return carry

        lax.fori_loop(1, n_grp, to_grp, 0)
        if more:
            take(kap_in.at[k], kap_sem.at[k])
            gather_coarse(k + 1, part + kap_in[k] * has_prev)
        take(dot_grp.at[k, pl.ds(0, n_grp - 1)], grp_sem.at[k])
        dots = jnp.sum(dot_grp[k], axis=0)
        dot_mid[k] = dots
        dot_sub[k, pl.ds(s, 1)] = dots[None]

        def to_sub(j, carry):
            remote(dot_mid.at[k], dot_sub.at[k, s], send_sem.at[9, k], sub_sem.at[k], lax.rem(s + j, n_sub), g).start()
            return carry

        lax.fori_loop(1, n_sub, to_sub, 0)
        if more:
            moved, moved_next = solve_coarse(k + 1)
        take(arrive.at[k, pl.ds(0, face)], bulk_sem.at[k, 0])
        if more:
            take(arrive.at[k, pl.ds(face, face)], bulk_sem.at[k, 1])
        take(dot_sub.at[k, pl.ds(0, n_sub - 1)], sub_sem.at[k])
        dots = jnp.sum(dot_sub[k], axis=0)
        gamma_now, delta_now, eps_now = dots[0:1], dots[1:2], dots[2:3]
        if k == 0:
            p_ap = delta_now
            beta = None
        else:
            beta = gamma_now / gamma_old
            p_ap = delta_now + beta * (2.0 * eps_now + beta * p_ap)
        alpha = gamma_now / p_ap
        gamma_old = gamma_now
        if more:
            drift = moved if k == 0 else moved + beta * drift
            drift_next = moved_next if k == 0 else moved_next + beta * drift_next
            solved = solved - alpha * drift
            solved_next = solved_next - alpha * drift_next
            stage_spread(0, solved)
            stage_spread(1, solved_next)

        def advance(span, came):
            fr = free[span]
            w = fr * (prod[span] + came) + (1.0 - fr) * zed[span]
            sr = w if k == 0 else w + beta * srch[span]
            return sr, res[span] - alpha * sr

        def own_rows(i, carry):
            gamma, delta, eps = carry
            span = place(i * CH)
            sr, r = advance(span, arrive[k, span].astype(F32) * has_prev)
            d = zed[span] if k == 0 else zed[span] + beta * direc[span]
            x = alpha * d if k == 0 else x_ref[span] + alpha * d
            x_ref[span] = x
            if not more:
                r_ref[span] = r
                return carry
            direc[span] = d
            srch[span] = sr
            res[span] = r
            z, fz = build(span, 0, r)
            rest = z - fz
            if k + 2 < ITERS:
                leftover(span, rest)
            return gamma + folded(r * z), delta + folded(rest * z), eps + folded(z * sr)

        gamma, delta, eps = lax.fori_loop(0, face // CH, own_rows, (zero8, zero8, zero8))
        if more:
            def next_rows(i, carry):
                span = place(face + i * CH)
                sr, r = advance(span, arrive[k, span].astype(F32))
                srch[span] = sr
                res[span] = r
                build(span, 1, r)
                return carry

            lax.fori_loop(0, face // CH, next_rows, 0)

    for k in range(ITERS):
        take(coarse_all.at[k, 0, pl.ds(0, n_sub - 1)], send_sem.at[0, k])
        take(coarse_src.at[k], send_sem.at[1, k])
        take(leave.at[k, pl.ds(face, face)], send_sem.at[6, k])
        if k + 1 < ITERS:
            take(leave.at[k, pl.ds(0, face)], send_sem.at[7, k])
            take(kap_src.at[k], send_sem.at[5, k])
        take(dot_grp.at[k, pl.ds(0, n_grp - 1)], send_sem.at[8, k])
        take(dot_sub.at[k, pl.ds(0, n_sub - 1)], send_sem.at[9, k])
    take(own_par, send_sem.at[2, 0])
    take(inv.at[0], send_sem.at[3, 0])
    take(half_b, send_sem.at[4, 0])


def solution(mesh):
    n_sub, n_grp = mesh.shape["sub"], mesh.shape["grp"]

    def local(right_side, schur_blocks, occupancy, precond_weights, coarse_basis, coarse_inverse):
        face, goals = right_side.shape[2:]
        nc = coarse_basis.shape[2]
        both = 2 * face
        dma = pltpu.SemaphoreType.DMA
        out = jax.ShapeDtypeStruct((face, goals), F32)
        x, r = pl.pallas_call(
            functools.partial(kernel, n_sub, n_grp),
            out_shape=(out, out),
            in_specs=[pl.BlockSpec(memory_space=pl.ANY)] * 6,
            out_specs=[pl.BlockSpec(memory_space=pltpu.VMEM)] * 2,
            scratch_shapes=[
                pltpu.VMEM((both, both), BF16),
                pltpu.VMEM((both, goals), F32),
                pltpu.VMEM((both, goals), F32),
                pltpu.VMEM((both, goals), F32),
                pltpu.VMEM((both, goals), F32),
                pltpu.VMEM((both, goals), F32),
                pltpu.VMEM((both, goals), F32),
                pltpu.VMEM((both, 2 * goals), BF16),
                pltpu.VMEM((face, goals), BF16),
                pltpu.VMEM((ITERS, both, goals), BF16),
                pltpu.VMEM((ITERS, both, goals), BF16),
                pltpu.VMEM((face, goals), BF16),
                pltpu.VMEM((nc + 8, face), F32),
                pltpu.VMEM((nc + 8, face), F32),
                pltpu.VMEM((1, face), jnp.int32),
                pltpu.VMEM((2, nc, n_sub * nc), F32),
                pltpu.VMEM((both, 4 * nc), BF16),
                pltpu.VMEM((2, 4 * nc, goals), BF16),
                pltpu.VMEM((face, 2 * goals), BF16),
                pltpu.VMEM((2, 2 * nc, both), BF16),
                pltpu.VMEM((2 * nc, face), BF16),
                pltpu.VMEM((face, goals), F32),
                pltpu.VMEM((ITERS, nc, goals), F32),
                pltpu.VMEM((ITERS, 2, n_sub, nc, goals), F32),
                pltpu.VMEM((ITERS, nc, goals), F32),
                pltpu.VMEM((ITERS, nc, goals), F32),
                pltpu.VMEM((ITERS, 4, goals), F32),
                pltpu.VMEM((ITERS, n_grp, 4, goals), F32),
                pltpu.VMEM((ITERS, 4, goals), F32),
                pltpu.VMEM((ITERS, n_sub, 4, goals), F32),
                dma((6,)),
                dma((10, ITERS)),
                dma,
                dma,
                dma,
                dma((ITERS, 2)),
                dma((ITERS,)),
                dma((ITERS,)),
                dma((ITERS,)),
                dma((ITERS,)),
                dma((ITERS,)),
            ],
            compiler_params=pltpu.CompilerParams(
                collective_id=0, has_side_effects=True, vmem_limit_bytes=48 << 20
            ),
        )(right_side[0, 0], schur_blocks[0, 0], occupancy[0], precond_weights[0], coarse_basis[0, 0], coarse_inverse[0])
        return x[None, None], r[None, None]

    return jax.shard_map(
        local,
        mesh=mesh,
        in_specs=(
            P("grp", "sub", None, None),
            P("grp", "sub", None, None),
            P("grp", "sub", None),
            P("grp", "sub", None),
            P("grp", "sub", None, None),
            P("grp", "sub", None),
        ),
        out_specs=(P("grp", "sub", None, None), P("grp", "sub", None, None)),
        check_vma=False,
    )
```

time: 649 us -> 87.6 us (0.13)
  blocking collectives: 537 us -> 0 us
  Pallas kernels: 0 us -> 81.1 us
  waiting for transfers between devices: 58.5 us -> 0 us
  matrix products: 25.7 us -> 0 us
  starting transfers between devices: 15.9 us -> 0 us
    psum x5 -> x0, blocking collectives: 403 us -> none  [the longest x3 232 us: precond_inner(): return lax.psum(jnp.sum(residual * precond, axis=0), ('sub', 'grp'))]
    all_gather x3 -> x0, blocking collectives: 134 us -> none  [precondition(): group_coarse = lax.all_gather(coarse, 'sub', axis=0, tiled=True)]
    pallas_call x0 -> x1, Pallas kernels: none -> 81.1 us  [local(): pl.pallas_call(functools.partial(kernel, n_sub, n_grp), out_shape=(out, o...]
    ppermute x12 -> x0, waiting for transfers between devices: 58.5 us -> none  [the longest x6 32.9 us: shifted(): lax.ppermute(value, axis, [(source, source + steps) for source in range(i...]
    dot_general x12 -> x0, matrix products: 25.7 us -> none  [the longest x3 18.8 us: local(): product = jnp.dot(schur_block, stacked, preferred_element_type=jnp.float32)]
    ppermute x12 -> x0, starting transfers between devices: 15.9 us -> none  [the longest x6 11 us: shifted(): lax.ppermute(value, axis, [(source, source + steps) for source in range(i...]
  transfers between devices with their start and end apart: 12 -> 0, of which waited for: 12 -> 0; matrix products, arithmetic and copies ran while one was open for 0% -> 0% of each run, Pallas kernels for 0% -> 0%
where the time goes in v1:
time: 87.6 us; the launch traced here: 87.2 us
  Pallas kernels  81.1 us (93%)
  local copies, waits for them, and re-layouts  5.45 us (6%)
    pallas_call x1, Pallas kernels, local(): pl.pallas_call(functools.partial(kernel, n_sub, n_grp), out_shape=(out, o...  81.1 us
    unnamed x12, local copies, waits for them, and re-layouts  5.45 us

profile of v1, /device:TPU:1, one launch (start us, length us, event | category | flops | bytes accessed | tf_op | source)
XLA Modules:
  0.0 87.2 jit_solution(13256692636044472818)
XLA Ops:
  0.6 0.0 copy-start
  0.6 1.0 %copy-done = f32[1,1,1024,128]{3,2,1,0:T(8,128)S(1)} copy-done((f32[1,1,1024,128]{3,2,1,0:T(8,128)S(1)}, f32[1,1,1024,128]{3,2,1,0:T(8,128)}, u32[]{:S(2)}) %copy-start) | copy-done | bytes 524312
  1.7 0.0 copy-start.1
  1.7 0.8 copy-done.1
  2.4 0.0 copy-start.2
  2.4 0.7 copy-done.2
  3.1 0.0 copy-start.3
  3.1 0.7 copy-done.3
  3.8 0.0 copy-start.4
  3.8 0.7 copy-done.4
  4.5 81.1 %shard_map.77 = (f32[1024,128]{1,0:T(8,128)S(1)}, f32[1024,128]{1,0:T(8,128)S(1)}) custom-call(f32[1024,128]{1,0:T(8,128)S(1)} %bitcast.8, bf16[2048,2048]{1,0:T(8,128)(2,1)} %bitcast.15, s32[1,1024]{1,0:T(1,128)S(1)} %bitcast.13, f32[1,1024]{1,0:T(1,128)S(1)} %bitcast.14, f32[8,1024]{1,0:T(8,128)S(1)} %bitcast.11, f32[8,256]{1,0:T(8,128)S(1)} %bitcast.12), custom_call_target="tpu_custom_call" | custom-call | tf_op jit(solution)/shard_map/pallas_call | solution.py:376
  85.6 0.8 copy.10
  86.4 0.8 copy.11
Async XLA Ops:
  0.6 1.0 %copy-start = (f32[1,1,1024,128]{3,2,1,0:T(8,128)S(1)}, f32[1,1,1024,128]{3,2,1,0:T(8,128)}, u32[]{:S(2)}) copy-start(f32[1,1,1024,128]{3,2,1,0:T(8,128)} %param.6) | copy-start | bytes 1572868
  1.7 0.8 copy-start.1
  2.4 0.7 copy-start.2
  3.1 0.7 copy-start.3
  3.8 0.7 copy-start.4

commit v2 on v1

--- a/solution.py
+++ b/solution.py
@@ -12,6 +12,9 @@
 F32 = jnp.float32
 BF16 = jnp.bfloat16
 CH = 256
+PLANE = 8
+CORES = 2
+ROW = 4
 
 
 def split(value):
@@ -30,11 +33,12 @@
 def kernel(
     n_sub, n_grp,
     b_hbm, s_hbm, occ_hbm, w_hbm, basis_hbm, inv_hbm,
+    x_out, r_out,
     x_ref, r_ref,
     blocks, res, zed, srch, prod, weight, free, masked, held, arrive, leave, half_b,
-    own_par, next_par, occ_v, inv, basis_t, spread_rhs, prob, qmat, basis_n, direc,
+    own_par, next_par, occ_v, weight_v, inv, basis_t, spread_rhs, prob, qmat, basis_n, basis_f, alone, qsum, qcol, solved_rhs, direc,
     coarse_src, coarse_all, kap_src, kap_in, dot_src, dot_grp, dot_mid, dot_sub,
-    load_sem, send_sem, par_sem, half_sem, inv_sem, bulk_sem, kap_sem, all_sem, far_sem, grp_sem, sub_sem,
+    load_sem, send_sem, par_sem, half_sem, inv_sem, bulk_sem, kap_sem, all_sem, far_sem, grp_sem, sub_sem, out_sem, swap_sem,
 ):
     s = lax.axis_index("sub")
     g = lax.axis_index("grp")
@@ -60,7 +64,7 @@
     loads = [
         local(b_hbm, res.at[pl.ds(0, face)], 0),
         local(occ_hbm, occ_v, 1),
-        local(w_hbm, own_par.at[pl.ds(nc, 1)], 2),
+        local(w_hbm, weight_v, 2),
         local(basis_hbm, own_par.at[pl.ds(0, nc)], 3),
         local(inv_hbm, inv.at[0], 4),
         local(s_hbm, blocks, 5),
@@ -77,16 +81,34 @@
         greet(lax.rem(s + j, n_sub), g)
         return carry
 
-    def greet_grp(j, carry):
-        greet(s, lax.rem(g + j, n_grp))
+    corner = g // ROW * ROW
+    n_near = PLANE * ROW
+    n_far = n_sub * n_grp // n_near
+    core = lax.rem(s, PLANE)
+    my_near = core * ROW + g - corner
+    my_far = s // PLANE * (n_grp // ROW) + g // ROW
+
+    def near(j):
+        i = lax.rem(my_near + j, n_near)
+        return s - core + i // ROW, corner + lax.rem(i, ROW)
+
+    def far(j):
+        i = lax.rem(my_far + j, n_far)
+        return i // (n_grp // ROW) * PLANE + core, lax.rem(i, n_grp // ROW) * ROW + g - corner
+
+    def greet_near(j, carry):
+        greet(*near(j))
+        return carry
+
+    def greet_far(j, carry):
+        greet(*far(j))
         return carry
 
     lax.fori_loop(1, n_sub, greet_sub, 0)
-    lax.fori_loop(1, n_grp, greet_grp, 0)
-
-    @pl.when(s != last_s)
-    def _():
-        greet(last_s, below_g)
+    lax.fori_loop(1, n_near, greet_near, 0)
+    lax.fori_loop(1, n_far, greet_far, 0)
+
+    greet(last_s, below_g)
 
     @pl.when(at_end)
     def _():
@@ -94,7 +116,7 @@
             greet(j, above_g)
             return carry
 
-        lax.fori_loop(0, last_s, greet_above, 0)
+        lax.fori_loop(0, n_sub, greet_above, 0)
 
     def remote(src, dst, send, recv, sub, grp):
         return pltpu.make_async_remote_copy(
@@ -105,26 +127,46 @@
     def take(ref, sem):
         pltpu.make_async_copy(ref, ref, sem).wait()
 
+    chips = n_sub // CORES
+    side = lax.rem(s, CORES)
+    chip = s // CORES
+    mine = pl.ds(side * chips, chips)
+
     def gather_coarse(k, value):
         coarse_src[k] = value
-        coarse_all[k, 0, pl.ds(s, 1)] = value[None]
+        coarse_all[k, 0, pl.ds(side * chips + chip, 1)] = value[None]
 
         def one(j, carry):
-            remote(coarse_src.at[k], coarse_all.at[k, 0, s], send_sem.at[0, k], all_sem.at[k], lax.rem(s + j, n_sub), g).start()
+            remote(
+                coarse_src.at[k], coarse_all.at[k, 0, side * chips + chip], send_sem.at[0, k], all_sem.at[k],
+                lax.rem(chip + j, chips) * CORES + side, g,
+            ).start()
             return carry
 
-        lax.fori_loop(1, n_sub, one, 0)
-        remote(coarse_src.at[k], coarse_all.at[k, 1, s], send_sem.at[1, k], far_sem.at[k], last_s, below_g).start()
+        lax.fori_loop(1, chips, one, 0)
+        remote(
+            coarse_src.at[k], coarse_all.at[k, 1, side * chips + chip], send_sem.at[1, k], far_sem.at[k], last_s, below_g
+        ).start()
+
+    def swap_coarse(k):
+        take(coarse_all.at[k, 0, pl.ds(0, chips - 1)], all_sem.at[k])
+        remote(
+            coarse_all.at[k, 0, mine], coarse_all.at[k, 0, mine], send_sem.at[10, k], swap_sem.at[k], s + 1 - 2 * side, g
+        ).start()
 
     def solve_coarse(k):
-        take(coarse_all.at[k, 0, pl.ds(0, n_sub - 1)], all_sem.at[k])
+        take(coarse_all.at[k, 0, mine], swap_sem.at[k])
 
         @pl.when(at_end)
         def _():
             take(coarse_all.at[k, 1], far_sem.at[k])
 
-        own = coarse_all[k, 0].reshape(n_sub * nc, goals)
-        beside = coarse_all[k, jnp.where(at_end, 1, 0)].reshape(n_sub * nc, goals)
+        def in_order(blocks_of):
+            parts = [blocks_of[i * chips:(i + 1) * chips] for i in range(CORES)]
+            return jnp.stack(parts, axis=1).reshape(n_sub * nc, goals)
+
+        own = in_order(coarse_all[k, 0])
+        beside = in_order(coarse_all[k, jnp.where(at_end, 1, 0)])
         dot = functools.partial(jnp.dot, precision=lax.Precision.HIGHEST, preferred_element_type=F32)
         return dot(inv[0], own), dot(inv[1], beside)
 
@@ -132,7 +174,7 @@
     loads[1].wait()
     loads[2].wait()
     loads[3].wait()
-    own_par[pl.ds(nc + 1, 1)] = occ_v[...].astype(F32)
+    own_par[pl.ds(nc, 8)] = jnp.concatenate([weight_v[...], occ_v[...].astype(F32), jnp.zeros((6, face), F32)], axis=0)
 
     def split_rows(rows):
         high, low = split(rows)
@@ -150,44 +192,84 @@
         return both[:rows] + both[rows:]
 
     first_coarse = unsplit(coarse, nc)
-    pl.semaphore_wait(barrier, (n_sub - 1) + (n_grp - 1) + jnp.where(at_end, n_sub - 1, 1))
-    gather_coarse(0, first_coarse)
+
+    line = lax.broadcasted_iota(jnp.int32, (8 * nc, 2 * goals), 0)
+    lane = lax.broadcasted_iota(jnp.int32, (8 * nc, 2 * goals), 1)
+    is_weight = jnp.logical_and(line >= 6 * nc, jnp.logical_and(line < 6 * nc + 3, lane < goals))
+    is_free = jnp.logical_and(line == 6 * nc + 3, lane >= goals)
+    pick = jnp.logical_or(is_weight, is_free).astype(F32).astype(BF16)
+
+    def prepare(base, params):
+        basis, wrow, frow = params[0:nc], params[nc:nc + 1], params[nc + 1:nc + 2]
+        high, low = split(basis)
+        fhigh, flow = split(basis * frow)
+        whigh = wrow.astype(BF16).astype(F32)
+        wmid = (wrow - whigh).astype(BF16).astype(F32)
+        rest = [whigh, wmid, wrow - whigh - wmid, frow]
+        tall = [high, high, low, low, fhigh, flow]
+        tall = jnp.concatenate([t.astype(F32) for t in tall] + rest + [jnp.zeros((2 * nc - 4, face), F32)], axis=0)
+        for col in range(0, face, 128):
+            span = pl.ds(base + col, 128)
+            cols = jnp.transpose(tall[:, col:col + 128]).astype(BF16)
+            basis_t[span] = cols
+            both = jnp.dot(cols, pick, preferred_element_type=F32)
+            weight[span] = both[:, :goals]
+            free[span] = both[:, goals:]
+            some, none = cols[:, 4 * nc:6 * nc], jnp.zeros((128, 2 * nc), BF16)
+            basis_f[span] = jnp.concatenate([some, none] if base == 0 else [none, some], axis=1)
+
+    params = own_par[...]
+    prepare(0, params)
+    basis_n[...] = split_rows(params[0:nc] * (1.0 - params[nc + 1:nc + 2]))
+
+    def weighted(i, span):
+        high, low = split(free[span] * (weight[span] * res[span]))
+        here = place(i * CH)
+        alone[here, 0:goals] = high
+        alone[here, goals:2 * goals] = low
+
+    def weighted_own(i, carry):
+        weighted(i, place(i * CH))
+        return carry
+
+    lax.fori_loop(0, face // CH, weighted_own, 0)
+    loads[5].wait()
+
+    def half_own(i, carry):
+        span = place(i * CH)
+        left = blocks[span, 0:face]
+        y = jnp.dot(left, alone[...], preferred_element_type=F32)
+        prod[span] = y[:, :goals] + y[:, goals:]
+        qsum[span] = jnp.dot(left, basis_f[0:face], preferred_element_type=F32)
+        return carry
+
+    lax.fori_loop(0, 2 * face // CH, half_own, 0)
+    pl.semaphore_wait(barrier, (n_sub - 1) + (n_near - 1) + (n_far - 1) + jnp.where(at_end, n_sub + 1, 1))
     remote(own_par, next_par, send_sem.at[2, 0], par_sem, prev_s, prev_g).start()
     loads[4].wait()
     remote(inv.at[0], inv.at[1], send_sem.at[3, 0], inv_sem, prev_s, prev_g).start()
     remote(half_b, held, send_sem.at[4, 0], half_sem, prev_s, prev_g).start()
-
-    def prepare(base, params):
-        high, low = split(params[0:nc])
-        quad = jnp.concatenate([high, high, low, low], axis=0).astype(F32)
-        for col in range(0, face, 128):
-            span = pl.ds(base + col, 128)
-            basis_t[span] = jnp.transpose(quad[:, col:col + 128]).astype(BF16)
-            weight[span] = jnp.transpose(jnp.broadcast_to(params[nc:nc + 1, col:col + 128], (128, 128)))
-            free[span] = jnp.transpose(jnp.broadcast_to(params[nc + 1:nc + 2, col:col + 128], (128, 128)))
-
-    def through(base, params, which):
-        rows = split_rows(params[0:nc] * params[nc + 1:nc + 2])
-        for col in range(0, 2 * face, CH):
-            out = jnp.dot(rows, blocks[pl.ds(base, face), pl.ds(col, CH)], preferred_element_type=F32)
-            high, low = split(out[:nc] + out[nc:])
-            qmat[which, 0:nc, pl.ds(col, CH)] = high
-            qmat[which, nc:2 * nc, pl.ds(col, CH)] = low
-
-    params = own_par[...]
-    prepare(0, params)
-    basis_n[...] = split_rows(params[0:nc] * (1.0 - params[nc + 1:nc + 2]))
-    loads[5].wait()
-    through(0, params, 0)
+    gather_coarse(0, first_coarse)
     take(next_par, par_sem)
-    params = next_par[...] * has_next
-    prepare(face, params)
-    through(face, params, 1)
+    prepare(face, next_par[...] * has_next)
+
+    def through(i, carry):
+        span = place(i * CH)
+        out = qsum[span] + jnp.dot(blocks[span, face:2 * face], basis_f[face:2 * face], preferred_element_type=F32)
+        out = jnp.transpose(out)
+        high, low = split(jnp.concatenate([out[0:nc] + out[nc:2 * nc], out[2 * nc:3 * nc] + out[3 * nc:]], axis=0))
+        qmat[:, span] = jnp.concatenate([high, low], axis=0)
+        high, low = high.astype(F32), low.astype(F32)
+        qcol[span] = jnp.transpose(jnp.concatenate([high, high, low, low], axis=0)).astype(BF16)
+        return carry
+
+    lax.fori_loop(0, 2 * face // CH, through, 0)
+    swap_coarse(0)
     take(inv.at[1], inv_sem)
 
     def stage_spread(which, value):
         high, low = split(value)
-        spread_rhs[which] = jnp.concatenate([high, low, high, low], axis=0)
+        spread_rhs[which] = jnp.concatenate([high, low, high, low, jnp.zeros((4 * nc, goals), BF16)], axis=0)
 
     def build(span, which, r):
         z = weight[span] * r + jnp.dot(basis_t[span], spread_rhs[which], preferred_element_type=F32)
@@ -202,6 +284,8 @@
     solved, solved_next = solve_coarse(0)
     stage_spread(0, solved)
     stage_spread(1, solved_next)
+    high, low = split(jnp.concatenate([solved, solved_next], axis=0))
+    solved_rhs[...] = jnp.concatenate([high, low, high, low], axis=0)
 
     def leftover(span, rest):
         high, low = split(rest)
@@ -226,6 +310,7 @@
         r = held[place(i * CH)].astype(F32) * has_next
         res[span] = r
         build(span, 1, r)
+        weighted(i, span)
         return carry
 
     lax.fori_loop(0, face // CH, first_next, 0)
@@ -235,18 +320,23 @@
     for k in range(ITERS):
         more = k + 1 < ITERS
         if more:
-            m_all = masked[...]
-            part = jnp.dot(qmat[0], m_all, preferred_element_type=F32)
-            kap = jnp.dot(qmat[1], m_all, preferred_element_type=F32)
-            part += jnp.dot(basis_n[...], prob[...], preferred_element_type=F32)
-            kap_src[k] = unsplit(kap, nc)
+            out = jnp.dot(qmat[...], masked[...], preferred_element_type=F32)
+            part = jnp.dot(basis_n[...], prob[...], preferred_element_type=F32)
+            out = out[:, :goals] + out[:, goals:]
+            out = out[:2 * nc] + out[2 * nc:]
+            kap_src[k] = out[nc:]
             remote(kap_src.at[k], kap_in.at[k], send_sem.at[5, k], kap_sem.at[k], next_s, next_g).start()
-            part = unsplit(part, nc)
+            part = unsplit(part, nc) + out[:nc]
 
         def rows_of(row, acc):
             span = place(row)
-            y = jnp.dot(blocks[span], masked[...], preferred_element_type=F32)
-            y = y[:, :goals] + y[:, goals:]
+            if k == 0:
+                y = jnp.dot(blocks[span, face:2 * face], alone[...], preferred_element_type=F32)
+                y = prod[span] + y[:, :goals] + y[:, goals:]
+                y += jnp.dot(qcol[span], solved_rhs[...], preferred_element_type=F32)
+            else:
+                y = jnp.dot(blocks[span], masked[...], preferred_element_type=F32)
+                y = y[:, :goals] + y[:, goals:]
             prod[span] = y
             leave[k, span] = y.astype(BF16)
             return acc + folded(free[span] * zed[span] * y)
@@ -269,32 +359,42 @@
         dots = [jnp.sum(v, axis=0, keepdims=True) for v in (gamma, delta, eps)]
         dots = jnp.concatenate(dots + [jnp.zeros((1, goals), F32)], axis=0)
         dot_src[k] = dots
-        dot_grp[k, pl.ds(g, 1)] = dots[None]
+        dot_grp[k, pl.ds(my_near, 1)] = dots[None]
 
         def to_grp(j, carry):
-            remote(dot_src.at[k], dot_grp.at[k, g], send_sem.at[8, k], grp_sem.at[k], s, lax.rem(g + j, n_grp)).start()
+            remote(dot_src.at[k], dot_grp.at[k, my_near], send_sem.at[8, k], grp_sem.at[k], *near(j)).start()
             return carry
 
-        lax.fori_loop(1, n_grp, to_grp, 0)
+        lax.fori_loop(1, n_near, to_grp, 0)
         if more:
             take(kap_in.at[k], kap_sem.at[k])
             gather_coarse(k + 1, part + kap_in[k] * has_prev)
-        take(dot_grp.at[k, pl.ds(0, n_grp - 1)], grp_sem.at[k])
+        take(dot_grp.at[k, pl.ds(0, n_near - 1)], grp_sem.at[k])
         dots = jnp.sum(dot_grp[k], axis=0)
         dot_mid[k] = dots
-        dot_sub[k, pl.ds(s, 1)] = dots[None]
+        dot_sub[k, pl.ds(my_far, 1)] = dots[None]
 
         def to_sub(j, carry):
-            remote(dot_mid.at[k], dot_sub.at[k, s], send_sem.at[9, k], sub_sem.at[k], lax.rem(s + j, n_sub), g).start()
+            remote(dot_mid.at[k], dot_sub.at[k, my_far], send_sem.at[9, k], sub_sem.at[k], *far(j)).start()
             return carry
 
-        lax.fori_loop(1, n_sub, to_sub, 0)
+        lax.fori_loop(1, n_far, to_sub, 0)
         if more:
+            swap_coarse(k + 1)
             moved, moved_next = solve_coarse(k + 1)
         take(arrive.at[k, pl.ds(0, face)], bulk_sem.at[k, 0])
         if more:
             take(arrive.at[k, pl.ds(face, face)], bulk_sem.at[k, 1])
-        take(dot_sub.at[k, pl.ds(0, n_sub - 1)], sub_sem.at[k])
+
+        def apply(i, carry):
+            span = place(i * CH)
+            fr = free[span]
+            came = arrive[k, span].astype(F32) * jnp.where(i < face // CH, has_prev, 1.0)
+            prod[span] = fr * (prod[span] + came) + (1.0 - fr) * zed[span]
+            return carry
+
+        lax.fori_loop(0, (2 if more else 1) * face // CH, apply, 0)
+        take(dot_sub.at[k, pl.ds(0, n_far - 1)], sub_sem.at[k])
         dots = jnp.sum(dot_sub[k], axis=0)
         gamma_now, delta_now, eps_now = dots[0:1], dots[1:2], dots[2:3]
         if k == 0:
@@ -313,21 +413,21 @@
             stage_spread(0, solved)
             stage_spread(1, solved_next)
 
-        def advance(span, came):
-            fr = free[span]
-            w = fr * (prod[span] + came) + (1.0 - fr) * zed[span]
-            sr = w if k == 0 else w + beta * srch[span]
+        def advance(span):
+            sr = prod[span] if k == 0 else prod[span] + beta * srch[span]
             return sr, res[span] - alpha * sr
 
         def own_rows(i, carry):
             gamma, delta, eps = carry
             span = place(i * CH)
-            sr, r = advance(span, arrive[k, span].astype(F32) * has_prev)
+            sr, r = advance(span)
             d = zed[span] if k == 0 else zed[span] + beta * direc[span]
             x = alpha * d if k == 0 else x_ref[span] + alpha * d
             x_ref[span] = x
             if not more:
                 r_ref[span] = r
+                pltpu.make_async_copy(x_ref.at[span], x_out.at[span], out_sem.at[0, i]).start()
+                pltpu.make_async_copy(r_ref.at[span], r_out.at[span], out_sem.at[1, i]).start()
                 return carry
             direc[span] = d
             srch[span] = sr
@@ -342,7 +442,7 @@
         if more:
             def next_rows(i, carry):
                 span = place(face + i * CH)
-                sr, r = advance(span, arrive[k, span].astype(F32))
+                sr, r = advance(span)
                 srch[span] = sr
                 res[span] = r
                 build(span, 1, r)
@@ -350,18 +450,38 @@
 
             lax.fori_loop(0, face // CH, next_rows, 0)
 
+    for i in range(face // CH):
+        pltpu.make_async_copy(x_ref.at[pl.ds(i * CH, CH)], x_out.at[pl.ds(i * CH, CH)], out_sem.at[0, i]).wait()
+        pltpu.make_async_copy(r_ref.at[pl.ds(i * CH, CH)], r_out.at[pl.ds(i * CH, CH)], out_sem.at[1, i]).wait()
     for k in range(ITERS):
-        take(coarse_all.at[k, 0, pl.ds(0, n_sub - 1)], send_sem.at[0, k])
+        take(coarse_all.at[k, 0, pl.ds(0, chips - 1)], send_sem.at[0, k])
+        take(coarse_all.at[k, 0, mine], send_sem.at[10, k])
         take(coarse_src.at[k], send_sem.at[1, k])
         take(leave.at[k, pl.ds(face, face)], send_sem.at[6, k])
         if k + 1 < ITERS:
             take(leave.at[k, pl.ds(0, face)], send_sem.at[7, k])
             take(kap_src.at[k], send_sem.at[5, k])
-        take(dot_grp.at[k, pl.ds(0, n_grp - 1)], send_sem.at[8, k])
-        take(dot_sub.at[k, pl.ds(0, n_sub - 1)], send_sem.at[9, k])
+        take(dot_grp.at[k, pl.ds(0, n_near - 1)], send_sem.at[8, k])
+        take(dot_sub.at[k, pl.ds(0, n_far - 1)], send_sem.at[9, k])
     take(own_par, send_sem.at[2, 0])
     take(inv.at[0], send_sem.at[3, 0])
     take(half_b, send_sem.at[4, 0])
+
+
+def ship(x_in, r_in, x_out, r_out, held, sem):
+    moves = []
+    for which, (src, dst) in enumerate(((x_in, x_out), (r_in, r_out))):
+        for i in range(src.shape[0] // CH):
+            span = pl.ds(i * CH, CH)
+            inward = pltpu.make_async_copy(src.at[span], held.at[which, span], sem.at[0, which, i])
+            outward = pltpu.make_async_copy(held.at[which, span], dst.at[span], sem.at[1, which, i])
+            inward.start()
+            moves.append((inward, outward))
+    for inward, outward in moves:
+        inward.wait()
+        outward.start()
+    for inward, outward in moves:
+        outward.wait()
 
 
 def solution(mesh):
@@ -377,8 +497,10 @@
             functools.partial(kernel, n_sub, n_grp),
             out_shape=(out, out),
             in_specs=[pl.BlockSpec(memory_space=pl.ANY)] * 6,
-            out_specs=[pl.BlockSpec(memory_space=pltpu.VMEM)] * 2,
+            out_specs=[pl.BlockSpec(memory_space=pl.ANY)] * 2,
             scratch_shapes=[
+                pltpu.VMEM((face, goals), F32),
+                pltpu.VMEM((face, goals), F32),
                 pltpu.VMEM((both, both), BF16),
                 pltpu.VMEM((both, goals), F32),
                 pltpu.VMEM((both, goals), F32),
@@ -394,23 +516,29 @@
                 pltpu.VMEM((nc + 8, face), F32),
                 pltpu.VMEM((nc + 8, face), F32),
                 pltpu.VMEM((1, face), jnp.int32),
+                pltpu.VMEM((1, face), F32),
                 pltpu.VMEM((2, nc, n_sub * nc), F32),
+                pltpu.VMEM((both, 8 * nc), BF16),
+                pltpu.VMEM((2, 8 * nc, goals), BF16),
+                pltpu.VMEM((face, 2 * goals), BF16),
+                pltpu.VMEM((4 * nc, both), BF16),
+                pltpu.VMEM((2 * nc, face), BF16),
                 pltpu.VMEM((both, 4 * nc), BF16),
-                pltpu.VMEM((2, 4 * nc, goals), BF16),
                 pltpu.VMEM((face, 2 * goals), BF16),
-                pltpu.VMEM((2, 2 * nc, both), BF16),
-                pltpu.VMEM((2 * nc, face), BF16),
+                pltpu.VMEM((both, 4 * nc), F32),
+                pltpu.VMEM((both, 8 * nc), BF16),
+                pltpu.VMEM((8 * nc, goals), BF16),
                 pltpu.VMEM((face, goals), F32),
                 pltpu.VMEM((ITERS, nc, goals), F32),
                 pltpu.VMEM((ITERS, 2, n_sub, nc, goals), F32),
                 pltpu.VMEM((ITERS, nc, goals), F32),
                 pltpu.VMEM((ITERS, nc, goals), F32),
                 pltpu.VMEM((ITERS, 4, goals), F32),
-                pltpu.VMEM((ITERS, n_grp, 4, goals), F32),
+                pltpu.VMEM((ITERS, PLANE * ROW, 4, goals), F32),
                 pltpu.VMEM((ITERS, 4, goals), F32),
-                pltpu.VMEM((ITERS, n_sub, 4, goals), F32),
+                pltpu.VMEM((ITERS, n_sub * n_grp // (PLANE * ROW), 4, goals), F32),
                 dma((6,)),
-                dma((10, ITERS)),
+                dma((11, ITERS)),
                 dma,
                 dma,
                 dma,
@@ -420,11 +548,20 @@
                 dma((ITERS,)),
                 dma((ITERS,)),
                 dma((ITERS,)),
+                dma((2, face // CH)),
+                dma((ITERS,)),
             ],
             compiler_params=pltpu.CompilerParams(
-                collective_id=0, has_side_effects=True, vmem_limit_bytes=48 << 20
+                collective_id=0, has_side_effects=True, vmem_limit_bytes=60 << 20
             ),
         )(right_side[0, 0], schur_blocks[0, 0], occupancy[0], precond_weights[0], coarse_basis[0, 0], coarse_inverse[0])
+        x, r = pl.pallas_call(
+            ship,
+            out_shape=(out, out),
+            in_specs=[pl.BlockSpec(memory_space=pl.ANY)] * 2,
+            out_specs=[pl.BlockSpec(memory_space=pl.ANY)] * 2,
+            scratch_shapes=[pltpu.VMEM((2, face, goals), F32), dma((2, 2, face // CH))],
+        )(x, r)
         return x[None, None], r[None, None]
 
     return jax.shard_map(

time: 87.6 us -> 79.9 us (0.912)
  local copies, waits for them, and re-layouts: 5.45 us -> 0 us
  Pallas kernels: 81.1 us -> 79.1 us
    unnamed x12 -> x0, local copies, waits for them, and re-layouts: 5.45 us -> none
    pallas_call x1, Pallas kernels: 81.1 us -> 77 us  [local(): pl.pallas_call(functools.partial(kernel, n_sub, n_grp), out_shape=(out, o...]
    pallas_call x0 -> x1, Pallas kernels: none -> 2.09 us  [local(): pl.pallas_call(ship, out_shape=(out, out), in_specs=[pl.BlockSpec(memory_...]
where the time goes in v2:
time: 79.9 us; the launch traced here: 79.7 us
  Pallas kernels  79.1 us (99%)
    pallas_call x1, Pallas kernels, local(): pl.pallas_call(functools.partial(kernel, n_sub, n_grp), out_shape=(out, o...  77 us
    pallas_call x1, Pallas kernels, local(): pl.pallas_call(ship, out_shape=(out, out), in_specs=[pl.BlockSpec(memory_...  2.09 us

profile of v2, /device:TPU:1, one launch (start us, length us, event | category | flops | bytes accessed | tf_op | source)
XLA Modules:
  0.0 79.7 jit_solution(17488338161440916808)
XLA Ops:
  0.6 77.0 %shard_map.77 = (f32[1024,128]{1,0:T(8,128)}, f32[1024,128]{1,0:T(8,128)}) custom-call(f32[1024,128]{1,0:T(8,128)} %bitcast.9, bf16[2048,2048]{1,0:T(8,128)(2,1)} %bitcast.8, s32[1,1024]{1,0:T(1,128)} %bitcast.12, f32[1,1024]{1,0:T(1,128)} %bitcast.13, f32[8,1024]{1,0:T(8,128)} %bitcast.10, f32[8,256]{1,0:T(8,128)} %bitcast.11), custom_call_target="tpu_custom_call" | custom-call | tf_op jit(solution)/shard_map/pallas_call | solution.py:496
  77.7 2.1 %shard_map.78 = (f32[1024,128]{1,0:T(8,128)}, f32[1024,128]{1,0:T(8,128)}) custom-call(f32[1024,128]{1,0:T(8,128)} %get-tuple-element.6.x_in, f32[1024,128]{1,0:T(8,128)} %get-tuple-element.7.r_in), custom_call_target="tpu_custom_call" | custom-call | tf_op jit(solution)/shard_map/pallas_call | solution.py:558

commit v3 on v2

--- a/solution.py
+++ b/solution.py
@@ -12,6 +12,7 @@
 F32 = jnp.float32
 BF16 = jnp.bfloat16
 CH = 256
+TALL = 512
 PLANE = 8
 CORES = 2
 ROW = 4
@@ -26,8 +27,8 @@
     return jnp.sum(value.reshape(value.shape[0] // 8, 8, value.shape[1]), axis=0)
 
 
-def place(row):
-    return pl.ds(pl.multiple_of(row, CH), CH)
+def place(row, size=CH):
+    return pl.ds(pl.multiple_of(row, size), size)
 
 
 def kernel(
@@ -35,7 +36,7 @@
     b_hbm, s_hbm, occ_hbm, w_hbm, basis_hbm, inv_hbm,
     x_out, r_out,
     x_ref, r_ref,
-    blocks, res, zed, srch, prod, weight, free, masked, held, arrive, leave, half_b,
+    blocks, res, zed, tee, vee, srch, prod, weight, free, masked, held, arrive, leave, half_b,
     own_par, next_par, occ_v, weight_v, inv, basis_t, spread_rhs, prob, qmat, basis_n, basis_f, alone, qsum, qcol, solved_rhs, direc,
     coarse_src, coarse_all, kap_src, kap_in, dot_src, dot_grp, dot_mid, dot_sub,
     load_sem, send_sem, par_sem, half_sem, inv_sem, bulk_sem, kap_sem, all_sem, far_sem, grp_sem, sub_sem, out_sem, swap_sem,
@@ -77,8 +78,13 @@
     def greet(sub, grp):
         pl.semaphore_signal(barrier, inc=1, device_id={"sub": sub, "grp": grp}, device_id_type=MESH)
 
-    def greet_sub(j, carry):
-        greet(lax.rem(s + j, n_sub), g)
+    chips = n_sub // CORES
+    side = lax.rem(s, CORES)
+    chip = s // CORES
+    mine = pl.ds(side * chips, chips)
+
+    def greet_like(j, carry):
+        greet(lax.rem(chip + j, chips) * CORES + side, g)
         return carry
 
     corner = g // ROW * ROW
@@ -104,7 +110,9 @@
         greet(*far(j))
         return carry
 
-    lax.fori_loop(1, n_sub, greet_sub, 0)
+    greet(prev_s, prev_g)
+    greet(next_s, next_g)
+    lax.fori_loop(1, chips, greet_like, 0)
     lax.fori_loop(1, n_near, greet_near, 0)
     lax.fori_loop(1, n_far, greet_far, 0)
 
@@ -127,10 +135,6 @@
     def take(ref, sem):
         pltpu.make_async_copy(ref, ref, sem).wait()
 
-    chips = n_sub // CORES
-    side = lax.rem(s, CORES)
-    chip = s // CORES
-    mine = pl.ds(side * chips, chips)
 
     def gather_coarse(k, value):
         coarse_src[k] = value
@@ -244,12 +248,12 @@
         return carry
 
     lax.fori_loop(0, 2 * face // CH, half_own, 0)
-    pl.semaphore_wait(barrier, (n_sub - 1) + (n_near - 1) + (n_far - 1) + jnp.where(at_end, n_sub + 1, 1))
+    pl.semaphore_wait(barrier, 2 + (chips - 1) + (n_near - 1) + (n_far - 1) + jnp.where(at_end, n_sub + 1, 1))
     remote(own_par, next_par, send_sem.at[2, 0], par_sem, prev_s, prev_g).start()
+    gather_coarse(0, first_coarse)
+    remote(half_b, held, send_sem.at[4, 0], half_sem, prev_s, prev_g).start()
     loads[4].wait()
     remote(inv.at[0], inv.at[1], send_sem.at[3, 0], inv_sem, prev_s, prev_g).start()
-    remote(half_b, held, send_sem.at[4, 0], half_sem, prev_s, prev_g).start()
-    gather_coarse(0, first_coarse)
     take(next_par, par_sem)
     prepare(face, next_par[...] * has_next)
 
@@ -316,7 +320,6 @@
     lax.fori_loop(0, face // CH, first_next, 0)
 
     gamma_old = p_ap = None
-    drift = drift_next = None
     for k in range(ITERS):
         more = k + 1 < ITERS
         if more:
@@ -329,7 +332,7 @@
             part = unsplit(part, nc) + out[:nc]
 
         def rows_of(row, acc):
-            span = place(row)
+            span = place(row, TALL)
             if k == 0:
                 y = jnp.dot(blocks[span, face:2 * face], alone[...], preferred_element_type=F32)
                 y = prod[span] + y[:, :goals] + y[:, goals:]
@@ -342,20 +345,20 @@
             return acc + folded(free[span] * zed[span] * y)
 
         def pair(i, acc):
-            acc = rows_of(face + i * CH, acc)
+            acc = rows_of(face + i * TALL, acc)
             remote(
-                leave.at[k, place(face + i * CH)], arrive.at[k, place(i * CH)],
+                leave.at[k, place(face + i * TALL, TALL)], arrive.at[k, place(i * TALL, TALL)],
                 send_sem.at[6, k], bulk_sem.at[k, 0], next_s, next_g,
             ).start()
-            acc = rows_of(i * CH, acc)
+            acc = rows_of(i * TALL, acc)
             if more:
                 remote(
-                    leave.at[k, place(i * CH)], arrive.at[k, place(face + i * CH)],
+                    leave.at[k, place(i * TALL, TALL)], arrive.at[k, place(face + i * TALL, TALL)],
                     send_sem.at[7, k], bulk_sem.at[k, 1], prev_s, prev_g,
                 ).start()
             return acc
 
-        delta = lax.fori_loop(0, face // CH, pair, delta)
+        delta = lax.fori_loop(0, face // TALL, pair, delta)
         dots = [jnp.sum(v, axis=0, keepdims=True) for v in (gamma, delta, eps)]
         dots = jnp.concatenate(dots + [jnp.zeros((1, goals), F32)], axis=0)
         dot_src[k] = dots
@@ -382,18 +385,32 @@
         if more:
             swap_coarse(k + 1)
             moved, moved_next = solve_coarse(k + 1)
+            stage_spread(0, moved)
+            stage_spread(1, moved_next)
         take(arrive.at[k, pl.ds(0, face)], bulk_sem.at[k, 0])
         if more:
             take(arrive.at[k, pl.ds(face, face)], bulk_sem.at[k, 1])
 
-        def apply(i, carry):
+        def apply(span, came, which):
+            fr = free[span]
+            w = fr * (prod[span] + came) + (1.0 - fr) * zed[span]
+            if more:
+                vee[span] = weight[span] * w + jnp.dot(basis_t[span], spread_rhs[which], preferred_element_type=F32)
+            return w
+
+        def apply_own(i, carry):
             span = place(i * CH)
-            fr = free[span]
-            came = arrive[k, span].astype(F32) * jnp.where(i < face // CH, has_prev, 1.0)
-            prod[span] = fr * (prod[span] + came) + (1.0 - fr) * zed[span]
+            prod[span] = apply(span, arrive[k, span].astype(F32) * has_prev, 0)
             return carry
 
-        lax.fori_loop(0, (2 if more else 1) * face // CH, apply, 0)
+        def apply_next(i, carry):
+            span = place(face + i * CH)
+            apply(span, arrive[k, span].astype(F32), 1)
+            return carry
+
+        lax.fori_loop(0, face // CH, apply_own, 0)
+        if more:
+            lax.fori_loop(0, face // CH, apply_next, 0)
         take(dot_sub.at[k, pl.ds(0, n_far - 1)], sub_sem.at[k])
         dots = jnp.sum(dot_sub[k], axis=0)
         gamma_now, delta_now, eps_now = dots[0:1], dots[1:2], dots[2:3]
@@ -405,22 +422,24 @@
             p_ap = delta_now + beta * (2.0 * eps_now + beta * p_ap)
         alpha = gamma_now / p_ap
         gamma_old = gamma_now
-        if more:
-            drift = moved if k == 0 else moved + beta * drift
-            drift_next = moved_next if k == 0 else moved_next + beta * drift_next
-            solved = solved - alpha * drift
-            solved_next = solved_next - alpha * drift_next
-            stage_spread(0, solved)
-            stage_spread(1, solved_next)
-
-        def advance(span):
-            sr = prod[span] if k == 0 else prod[span] + beta * srch[span]
-            return sr, res[span] - alpha * sr
+
+        def turn(span):
+            t = vee[span] if k == 0 else vee[span] + beta * tee[span]
+            if k + 2 < ITERS:
+                tee[span] = t
+            z = zed[span] - alpha * t
+            zed[span] = z
+            fz = free[span] * z
+            high, low = split(fz)
+            masked[span, 0:goals] = high
+            masked[span, goals:2 * goals] = low
+            return z, z - fz
 
         def own_rows(i, carry):
             gamma, delta, eps = carry
             span = place(i * CH)
-            sr, r = advance(span)
+            sr = prod[span] if k == 0 else prod[span] + beta * srch[span]
+            r = res[span] - alpha * sr
             d = zed[span] if k == 0 else zed[span] + beta * direc[span]
             x = alpha * d if k == 0 else x_ref[span] + alpha * d
             x_ref[span] = x
@@ -432,8 +451,7 @@
             direc[span] = d
             srch[span] = sr
             res[span] = r
-            z, fz = build(span, 0, r)
-            rest = z - fz
+            z, rest = turn(span)
             if k + 2 < ITERS:
                 leftover(span, rest)
             return gamma + folded(r * z), delta + folded(rest * z), eps + folded(z * sr)
@@ -441,11 +459,7 @@
         gamma, delta, eps = lax.fori_loop(0, face // CH, own_rows, (zero8, zero8, zero8))
         if more:
             def next_rows(i, carry):
-                span = place(face + i * CH)
-                sr, r = advance(span)
-                srch[span] = sr
-                res[span] = r
-                build(span, 1, r)
+                turn(place(face + i * CH))
                 return carry
 
             lax.fori_loop(0, face // CH, next_rows, 0)
@@ -502,6 +516,8 @@
                 pltpu.VMEM((face, goals), F32),
                 pltpu.VMEM((face, goals), F32),
                 pltpu.VMEM((both, both), BF16),
+                pltpu.VMEM((both, goals), F32),
+                pltpu.VMEM((both, goals), F32),
                 pltpu.VMEM((both, goals), F32),
                 pltpu.VMEM((both, goals), F32),
                 pltpu.VMEM((both, goals), F32),

time: 79.9 us -> 77.5 us (0.970)
  Pallas kernels: 79.1 us -> 76.7 us
    pallas_call x1, Pallas kernels: 77 us -> 74.7 us  [local(): pl.pallas_call(functools.partial(kernel, n_sub, n_grp), out_shape=(out, o...]
where the time goes in v3:
time: 77.5 us; the launch traced here: 77.4 us
  Pallas kernels  76.7 us (99%)
    pallas_call x1, Pallas kernels, local(): pl.pallas_call(functools.partial(kernel, n_sub, n_grp), out_shape=(out, o...  74.7 us
    pallas_call x1, Pallas kernels, local(): pl.pallas_call(ship, out_shape=(out, out), in_specs=[pl.BlockSpec(memory_...  2.09 us

profile of v3, /device:TPU:1, one launch (start us, length us, event | category | flops | bytes accessed | tf_op | source)
XLA Modules:
  0.0 77.4 jit_solution(11310926485587740006)
XLA Ops:
  0.6 74.7 %shard_map.77 = (f32[1024,128]{1,0:T(8,128)}, f32[1024,128]{1,0:T(8,128)}) custom-call(f32[1024,128]{1,0:T(8,128)} %bitcast.9, bf16[2048,2048]{1,0:T(8,128)(2,1)} %bitcast.8, s32[1,1024]{1,0:T(1,128)} %bitcast.12, f32[1,1024]{1,0:T(1,128)} %bitcast.13, f32[8,1024]{1,0:T(8,128)} %bitcast.10, f32[8,256]{1,0:T(8,128)} %bitcast.11), custom_call_target="tpu_custom_call" | custom-call | tf_op jit(solution)/shard_map/pallas_call | solution.py:510
  75.3 2.1 %shard_map.78 = (f32[1024,128]{1,0:T(8,128)}, f32[1024,128]{1,0:T(8,128)}) custom-call(f32[1024,128]{1,0:T(8,128)} %get-tuple-element.6.x_in, f32[1024,128]{1,0:T(8,128)} %get-tuple-element.7.r_in), custom_call_target="tpu_custom_call" | custom-call | tf_op jit(solution)/shard_map/pallas_call | solution.py:574
